TPU v7x, 32 devices: a whole 2x2x4 slice. The times are simulated.
32 devices in a mesh: cand: 4 (over x, core), seq: 8 (over z, y).
Axes of the slice: x: 2, y: 2, z: 4, core: 2. Of those that a mesh axis runs over, the one named last changes fastest.
Arguments:
- latent: bfloat16 [4, 384, 3072], P('cand', 'seq'), may hold values from -0.59765625 to 0.59765625
- timesteps: int32 [4], replicated, may hold values from 0 to 999
- positions: int32 [3, 384], replicated, may hold values from 0 to 63
- mod_weight: bfloat16 [3072, 9216], P('cand', 'seq'), may hold values from -0.109375 to 0.109375
- input_weight: bfloat16 [3072, 16, 384], P('cand', 'seq'), may hold values from -0.109375 to 0.109375
- output_weight: bfloat16 [16, 128, 3072], P('seq', None, 'cand'), may hold values from -0.75 to 0.75
- cotangent: bfloat16 [4, 384, 3072], P('cand', 'seq'), may hold values from -6 to 6
Outputs:
- block_out: bfloat16 [4, 384, 3072], P('cand', 'seq')
- latent_grad: float32 [4, 384, 3072], P('cand', 'seq')
All inputs are finite; a program needn't handle non-finite values.
Results may differ from a plain program's by a relative error of at most 0.033.
Values may be sent and summed in bfloat16 or wider, within the bound.
A program may use at most 128 MiB of HBM per device.

v0:
```python
import jax
import jax.numpy as jnp
import numpy as np
from jax import lax
from jax.sharding import PartitionSpec as P

HEAD = 128
epsilon = 1e-06


def time_embed(timesteps, feature_width):
    half_size = feature_width // 2
    freq_rate = jnp.exp(-jnp.log(10000.0) * jnp.arange(half_size, dtype=jnp.float32) / half_size)
    angles = timesteps.astype(jnp.float32)[:, None] * freq_rate[None, :]
    return jnp.concatenate([jnp.cos(angles), jnp.sin(angles)], axis=1)


def rope_tables(positions, head_size):
    first_size = head_size // 8
    other_size = (head_size - first_size) // 2
    pieces = []
    swapped = []
    sign_vec = []
    offset = 0
    for axis_id, width_part in enumerate((first_size, other_size, other_size)):
        half_size = width_part // 2
        freq_rate = jnp.exp(
            -jnp.log(256.0) * 2.0 * jnp.arange(half_size, dtype=jnp.float32) / width_part
        )
        angle_part = positions[axis_id].astype(jnp.float32)[:, None] * freq_rate[None, :]
        pieces.append(angle_part)
        pieces.append(angle_part)
        swapped += list(range(offset + half_size, offset + width_part)) + list(
            range(offset, offset + half_size)
        )
        sign_vec += [-1.0] * half_size + [1.0] * half_size
        offset += width_part
    angles = jnp.concatenate(pieces, axis=1)
    return (
        jnp.cos(angles),
        jnp.sin(angles),
        np.array(swapped, np.int32),
        np.array(sign_vec, np.float32),
    )


def rotate(values, tables):
    cos_tab, sin_tab, swapped, sign_vec = tables
    return values * cos_tab + values[..., swapped] * sign_vec * sin_tab


def unrotate(values, tables):
    cos_tab, sin_tab, swapped, sign_vec = tables
    return values * cos_tab - (values * sin_tab)[..., swapped] * sign_vec


def rms_norm(values):
    inverse = lax.rsqrt(jnp.mean(values * values, -1, keepdims=True) + epsilon)
    return (values * inverse, inverse)


def rms_back(d_normed, normed, inverse):
    return inverse * (d_normed - normed * jnp.mean(d_normed * normed, -1, keepdims=True))


def layer_norm(values):
    centred = values - jnp.mean(values, -1, keepdims=True)
    inverse_std = lax.rsqrt(jnp.mean(centred * centred, -1, keepdims=True) + epsilon)
    return (centred * inverse_std, inverse_std)


def layer_norm_back(d_normed, normed, inverse_std):
    return inverse_std * (
        d_normed
        - jnp.mean(d_normed, -1, keepdims=True)
        - normed * jnp.mean(d_normed * normed, -1, keepdims=True)
    )


def times_transposed(left, right):
    return lax.dot_general(
        left, right, (((1,), (1,)), ((), ())), preferred_element_type=jnp.float32
    )


def attend(projected, tables):
    length, groups, triple = projected.shape
    head_size = triple // 3
    grouped = jnp.transpose(projected.reshape(length, groups, 3, head_size), (2, 1, 0, 3))
    query_n, query_inv = rms_norm(grouped[0])
    key_n, key_inv = rms_norm(grouped[1])
    q_rot = rotate(query_n, tables).astype(jnp.bfloat16)
    k_rot = rotate(key_n, tables).astype(jnp.bfloat16)
    values = grouped[2].astype(jnp.bfloat16)
    score_scale = head_size ** (-0.5)
    scores = (
        jnp.einsum("gld,gmd->glm", q_rot, k_rot, preferred_element_type=jnp.float32) * score_scale
    )
    weights = jnp.exp(scores - head_size**0.5)
    probs = weights / jnp.sum(weights, -1, keepdims=True)
    probs_low = probs.astype(jnp.bfloat16)
    heads_out = jnp.einsum("glm,gmd->gld", probs_low, values, preferred_element_type=jnp.float32)
    attended = (
        jnp.transpose(heads_out, (1, 0, 2)).reshape(length, groups * head_size).astype(jnp.bfloat16)
    )
    saved = (q_rot, k_rot, values, probs, probs_low, query_n, query_inv, key_n, key_inv)
    return (attended, saved)


def attend_back(d_attended, saved, tables):
    q_rot, k_rot, values, probs, probs_low, query_n, query_inv, key_n, key_inv = saved
    groups, length, head_size = q_rot.shape
    score_scale = head_size ** (-0.5)
    d_heads = jnp.transpose(d_attended.reshape(length, groups, head_size), (1, 0, 2))
    d_values = jnp.einsum("glm,gld->gmd", probs_low, d_heads, preferred_element_type=jnp.float32)
    d_probs = jnp.einsum("gld,gmd->glm", d_heads, values, preferred_element_type=jnp.float32)
    d_scores = (probs * (d_probs - jnp.sum(probs * d_probs, -1, keepdims=True))).astype(
        jnp.bfloat16
    )
    d_qrot = (
        jnp.einsum("glm,gmd->gld", d_scores, k_rot, preferred_element_type=jnp.float32)
        * score_scale
    )
    d_krot = (
        jnp.einsum("glm,gld->gmd", d_scores, q_rot, preferred_element_type=jnp.float32)
        * score_scale
    )
    d_query = rms_back(unrotate(d_qrot, tables), query_n, query_inv)
    d_key = rms_back(unrotate(d_krot, tables), key_n, key_inv)
    stacked = jnp.stack([d_query, d_key, d_values], 0)
    return (
        jnp.transpose(stacked, (2, 1, 0, 3))
        .reshape(length, groups * 3 * head_size)
        .astype(jnp.bfloat16)
    )


def on_device(latent, timesteps, positions, mod_weight, input_weight, output_weight, cotangent):
    width = latent.shape[2]
    groups = input_weight.shape[1]
    group_cols = groups * input_weight.shape[2]
    time_act = jax.nn.silu(time_embed(timesteps, width)).astype(jnp.bfloat16)
    slab_rows = mod_weight.shape[0]
    act_rows = lax.dynamic_slice_in_dim(time_act, lax.axis_index("cand") * slab_rows, slab_rows, 1)
    mod_mine = lax.psum_scatter(
        jnp.dot(act_rows, mod_weight, preferred_element_type=jnp.float32).astype(jnp.bfloat16),
        "cand",
        scatter_dimension=0,
        tiled=True,
    ).astype(jnp.float32)
    modulation = lax.all_gather(mod_mine, "seq", axis=1, tiled=True)[0]
    shift_vec = modulation[:width]
    scale_vec = modulation[width : 2 * width]
    gate_vec = modulation[2 * width :]
    latent_all = lax.all_gather(latent[0], "seq", axis=0, tiled=True)
    length = latent_all.shape[0]
    normed_all, _ = layer_norm(latent_all.astype(jnp.float32))
    modulated = (normed_all * (1.0 + scale_vec) + shift_vec).astype(jnp.bfloat16)
    tables = rope_tables(positions, HEAD)
    piece = lax.all_gather(input_weight, "cand", axis=0, tiled=True).reshape(width, group_cols)
    cot_all = lax.all_gather(cotangent[0], "seq", axis=0, tiled=True)
    w_heads = lax.all_gather(output_weight, "cand", axis=2, tiled=True)
    w_heads = w_heads.reshape(w_heads.shape[0] * w_heads.shape[1], width)
    projected = jnp.dot(modulated, piece, preferred_element_type=jnp.float32)
    attended, saved = attend(projected.reshape(length, groups, 3 * HEAD), tables)
    mixed_part = jnp.dot(attended, w_heads, preferred_element_type=jnp.float32).astype(jnp.bfloat16)
    mixed = lax.psum_scatter(mixed_part, "seq", scatter_dimension=0, tiled=True).astype(jnp.float32)
    latent_rows = latent[0].astype(jnp.float32)
    block_out = (latent_rows + gate_vec * mixed).astype(jnp.bfloat16)
    d_mixed = (cot_all.astype(jnp.float32) * gate_vec).astype(jnp.bfloat16)
    d_attended = times_transposed(d_mixed, w_heads).astype(jnp.bfloat16)
    d_projected = attend_back(d_attended, saved, tables)
    d_modulated = lax.psum_scatter(
        times_transposed(d_projected, piece).astype(jnp.bfloat16),
        "seq",
        scatter_dimension=0,
        tiled=True,
    ).astype(jnp.float32)
    normed, inverse_std = layer_norm(latent_rows)
    latent_grad = cotangent[0].astype(jnp.float32) + layer_norm_back(
        d_modulated * (1.0 + scale_vec), normed, inverse_std
    )
    return (block_out[None], latent_grad[None])


def solution(mesh):
    placed = (
        P("cand", "seq", None),
        P(),
        P(),
        P("cand", "seq"),
        P("cand", "seq", None),
        P("seq", None, "cand"),
        P("cand", "seq", None),
    )
    return jax.shard_map(
        on_device,
        mesh=mesh,
        in_specs=placed,
        out_specs=(P("cand", "seq", None), P("cand", "seq", None)),
        check_vma=False,
    )
```

profile of v0, /device:TPU:0, one launch (start us, length us, event | category | flops | bytes accessed | tf_op | source)
XLA Modules:
  0.0 379.9 jit_solution(7271335132875156814)
XLA Ops:
  11.9 8.7 %all-reduce = bf16[4,1152]{1,0:T(4,128)(2,1)S(1)} all-reduce(bf16[4,1152]{1,0:T(4,128)(2,1)S(1)} %convolution_convert_fusion.1), channel_id=4, replica_groups=mesh['cand'=4,'seq'=8] {'cand'}, use_global_device_ids=true, to_apply=%region_0.1.clone | all-reduce | flops 4608 | bytes 18432
  21.2 31.6 %all_gather.15 = f32[1,9216]{1,0:T(1,128)S(1)} all-gather(f32[1,1152]{1,0:T(1,128)S(1)} %dynamic-slice_convert_fusion), channel_id=1, replica_groups=mesh['cand'=4,'seq'=8] {'seq'}, dimensions={1}, use_global_device_ids=true | all-gather | bytes 41472 | tf_op jit(solution)/shard_map/all_gather | solution.py:151
  54.9 10.1 %all-gather.11.cloned.1.call-done = bf16[1,384,3072]{2,1,0:T(8,128)(2,1)} async-done(((bf16[1,48,3072]{2,1,0:T(8,128)(2,1)}), bf16[1,384,3072]{2,1,0:T(8,128)(2,1)}) %all-gather.11.cloned.1.call-update) | async-done | bytes 2359312 | tf_op jit(solution)/shard_map/all_gather | solution.py:155
  65.0 2.2 convert_reduce_fusion
  68.1 16.7 %all-gather.9.cloned.1.call-done = bf16[2,128,3072]{2,1,0:T(8,128)(2,1)} async-done(((bf16[2,128,768]{2,1,0:T(8,128)(2,1)}), bf16[2,128,3072]{2,1,0:T(8,128)(2,1)}) %all-gather.9.cloned.1.call-update) | async-done | bytes 1572880 | tf_op jit(solution)/shard_map/all_gather | solution.py:162
  84.8 54.0 %all-gather.13.cloned.1.call-done = bf16[1,384,3072]{2,1,0:T(8,128)(2,1)} async-done(((bf16[1,48,3072]{2,1,0:T(8,128)(2,1)}), bf16[1,384,3072]{2,1,0:T(8,128)(2,1)}) %all-gather.13.cloned.1.call-update) | async-done | bytes 2359312 | tf_op jit(solution)/shard_map/all_gather | solution.py:161
  138.9 3.1 fusion.24
  142.0 34.3 %all-gather.7.cloned.1.call-done = bf16[3072,2,384]{2,1,0:T(2,128)(2,1)} async-done(((bf16[768,2,384]{2,1,0:T(2,128)(2,1)}), bf16[3072,2,384]{2,1,0:T(2,128)(2,1)}) %all-gather.7.cloned.1.call-update) | async-done | bytes 4718608 | tf_op jit(solution)/shard_map/all_gather | solution.py:160
  176.3 5.3 %copy.73 = bf16[384,8,2,384]{3,1,2,0:T(8,128)(2,1)} copy(bf16[384,8,2,384]{3,2,1,0:T(2,128)(2,1)} %bitcast.164) | data formatting | bytes 9437184
  181.5 6.7 %copy.42 = bf16[3072,768]{0,1:T(8,128)(2,1)} copy(bf16[3072,768]{1,0:T(8,128)(2,1)} %bitcast.160) | data formatting | bytes 9437184 | tf_op jit(solution)/shard_map/reshape | solution.py:160
  188.3 5.5 %fusion.19 = f32[3,2,384,128]{2,3,0,1:T(8,128)S(1)} fusion(bf16[2,3,128,3072]{3,2,1,0:T(8,128)(2,1)} %bitcast.165, bf16[1,384,3072]{2,1,0:T(8,128)(2,1)} %all-gather.11.cloned.1.call-done, f32[3072]{0:T(1024)S(1)} %bitcast.175, f32[3072]{0:T(1024)S(1)} %bitcast.170, f32[384]{0:T(512)S(1)} %add_rsqrt_fusion.2, f32[384]{0:T(512)S(1)} %broadcast_multiply_fusion.9), kind=kOutput, calls=%fused_computation.27 | convolution fusion | flops 1819017216 | bytes 8285184 | tf_op jit(solution)/shard_map/dot_general | solution.py:164
  194.9 1.1 copy.44
  195.9 1.1 copy.46
  197.0 2.2 gather_fusion
  199.2 2.9 gather_fusion.1
  202.1 2.5 fusion.58
  204.5 1.6 fusion.46
  206.1 2.1 multiply_reduce_fusion
  208.2 2.0 fusion.28
  211.5 1.1 broadcast_multiply_fusion
  212.6 1.1 copy.58
  213.7 2.9 gather_fusion.3
  216.6 2.1 copy.55
  218.7 2.9 gather_fusion.2
  221.6 2.0 multiply_reduce_fusion.2
  224.4 0.9 slice-done.1
  225.3 3.5 convolution_convert_fusion
  228.9 4.0 %bitcast_convert_fusion = bf16[384,3072]{1,0:T(8,128)(2,1)} fusion(bf16[2,128,3072]{2,1,0:T(8,128)(2,1)} %all-gather.9.cloned.1.call-done, f32[2,384,384]{1,2,0:T(8,128)S(1)} %get-tuple-element.31, f32[3,2,384,128]{2,3,0,1:T(8,128)} %copy-done.10), kind=kOutput, calls=%fused_computation.15 | convolution fusion | flops 681050112 | bytes 5308416 | tf_op jit(solution)/shard_map/dot_general | solution.py:166
  234.3 64.3 %reduce-scatter.5.cloned.1.call-done = bf16[48,3072]{1,0:T(8,128)(2,1)} async-done(((bf16[384,3072]{1,0:T(8,128)(2,1)}), bf16[48,3072]{1,0:T(8,128)(2,1)}) %reduce-scatter.5.cloned.1.call-update) | async-done | bytes 294928 | tf_op jit(solution)/shard_map/reduce_scatter | solution.py:173
  298.6 1.2 fusion.42
  299.8 70.9 %reduce-scatter.3.cloned.1.call-done = bf16[48,3072]{1,0:T(8,128)(2,1)} async-done(((bf16[384,3072]{1,0:T(8,128)(2,1)}), bf16[48,3072]{1,0:T(8,128)(2,1)}) %reduce-scatter.3.cloned.1.call-update) | async-done | bytes 294928 | tf_op jit(solution)/shard_map/reduce_scatter | solution.py:167
  370.8 2.3 fusion.39
  (113 shorter events, 12.6 us)
Async XLA Ops:
  7.2 4.3 %copy-start = (bf16[768,1152]{1,0:T(8,128)(2,1)S(1)}, bf16[768,1152]{1,0:T(8,128)(2,1)}, u32[]{:S(2)}) copy-start(bf16[768,1152]{1,0:T(8,128)(2,1)} %param.16) | copy-start | bytes 5308420
  7.2 2.9 copy-start.30
  7.2 2.9 copy-start.29
  7.2 3.5 copy-start.27
  7.2 57.8 %all-gather.11.cloned.1.call-start = ((), (), s32[]{:S(2)}) async-start(), calls=%async_computation.6 | async-start | bytes 2654208 | tf_op jit(solution)/shard_map/all_gather | solution.py:155
  7.9 76.9 %all-gather.9.cloned.1.call-start = ((), (), s32[]{:S(2)}) async-start(), calls=%async_computation.3 | async-start | bytes 1966080 | tf_op jit(solution)/shard_map/all_gather | solution.py:162
  8.7 130.2 %all-gather.13.cloned.1.call-start = ((), (), s32[]{:S(2)}) async-start(), calls=%async_computation.7 | async-start | bytes 2654208 | tf_op jit(solution)/shard_map/all_gather | solution.py:161
  9.4 43.4 %copy-start.28 = (s32[128]{0:T(128)S(1)}, s32[128]{0:T(128)}, u32[]{:S(2)}) copy-start(s32[128]{0:T(128)} %constant.73) | copy-start | bytes 1540
  9.4 166.8 %all-gather.7.cloned.1.call-start = ((), (), s32[]{:S(2)}) async-start(), calls=%async_computation.2 | async-start | bytes 5898240 | tf_op jit(solution)/shard_map/all_gather | solution.py:160
  10.0 288.6 %reduce-scatter.5.cloned.1.call-start = ((), (), s32[]{:S(2)}) async-start(), calls=%async_computation.5 | async-start | bytes 2654208 | tf_op jit(solution)/shard_map/reduce_scatter | solution.py:173
  54.9 84.0 %copy-start.22 = (f32[1,3072]{1,0:T(1,128)}, f32[1,3072]{1,0:T(1,128)S(1)}, u32[]{:S(2)}) copy-start(f32[1,3072]{1,0:T(1,128)S(1)} %get-tuple-element.23) | copy-start | bytes 36868
  65.0 2.4 copy-start.5
  142.0 60.1 %copy-start.18 = (bf16[384,256]{0,1:T(8,128)(2,1)}, bf16[384,256]{0,1:T(8,128)(2,1)S(1)}, u32[]{:S(2)}) copy-start(bf16[384,256]{0,1:T(8,128)(2,1)S(1)} %fusion.24) | copy-start | bytes 589828
  193.9 2.1 copy-start.24
  194.9 11.2 %copy-start.3 = (f32[2,384,128]{1,2,0:T(8,128)}, f32[2,384,128]{1,2,0:T(8,128)S(1)}, u32[]{:S(2)}) copy-start(f32[2,384,128]{1,2,0:T(8,128)S(1)} %get-tuple-element.12) | copy-start | bytes 1179652
  194.9 13.3 %copy-start.1 = (f32[2,384,128]{1,2,0:T(8,128)}, f32[2,384,128]{1,2,0:T(8,128)S(1)}, u32[]{:S(2)}) copy-start(f32[2,384,128]{1,2,0:T(8,128)S(1)} %get-tuple-element.11) | copy-start | bytes 1179652
  202.1 2.5 copy-start.15
  212.6 9.0 %copy-start.26 = (f32[128]{0:T(128)S(1)}, f32[128]{0:T(128)}, u32[]{:S(2)}) copy-start(f32[128]{0:T(128)} %constant.67.clone) | copy-start | bytes 1540
  212.6 11.8 %slice-start = ((s8[4718592]{0:T(1024)(128)(4,1)}), s8[524288]{0:T(1024)(128)(4,1)S(1)}, s32[]{:S(2)}) async-start(s8[4718592]{0:T(1024)(128)(4,1)} %bitcast.161), calls=%async_computation.8 | async-start | bytes 1048576
  218.6 5.0 %copy-start.25 = (f32[2,384]{1,0:T(2,128)S(1)}, f32[2,384]{1,0:T(2,128)}, u32[]{:S(2)}) copy-start(f32[2,384]{1,0:T(2,128)} %copy-done.24) | copy-start | bytes 9220
  221.5 2.2 copy-start.2
  221.5 2.2 copy-start.4
  221.5 2.2 copy-start.8
  221.5 2.2 copy-start.11
  221.5 2.3 copy-start.12
  221.5 2.4 copy-start.13
  221.5 2.4 copy-start.14
  221.6 2.7 copy-start.17
  221.6 3.8 slice-start.1
  228.9 141.9 %reduce-scatter.3.cloned.1.call-start = ((), (), s32[]{:S(2)}) async-start(), calls=%async_computation.4 | async-start | bytes 2654208 | tf_op jit(solution)/shard_map/reduce_scatter | solution.py:167
  232.9 137.8 %copy-start.16 = (bf16[1,48,3072]{2,1,0:T(8,128)(2,1)S(1)}, bf16[1,48,3072]{2,1,0:T(8,128)(2,1)}, u32[]{:S(2)}) copy-start(bf16[1,48,3072]{2,1,0:T(8,128)(2,1)} %param.19) | copy-start | bytes 884740
  232.9 137.8 %copy-start.23 = (f32[1,3072]{1,0:T(1,128)S(1)}, f32[1,3072]{1,0:T(1,128)}, u32[]{:S(2)}) copy-start(f32[1,3072]{1,0:T(1,128)} %copy-done.22) | copy-start | bytes 36868
  (7 other events, 8.6 us)
Sparse Core Ops, SparseCore 0:
  10.2 54.7 all-gather.10
  66.5 18.2 all-gather.8
  87.0 51.8 all-gather.12
  140.3 35.9 all-gather.6
  229.0 69.5 reduce-scatter.4
  301.9 68.7 reduce-scatter.2
where the time goes:
time: 381 us; the launch traced here: 380 us
  waiting for transfers between devices  253 us (66%)
  blocking collectives  40.3 us (11%)
  local copies, waits for them, and re-layouts  33.8 us (9%)
  matrix products  24.5 us (6%)
  between operations  14.6 us (4%)
  other arithmetic  13.7 us (4%)
    reduce_scatter x1, waiting for transfers between devices, on_device(): lax.psum_scatter(mixed_part, 'seq', scatter_dimension=0, tiled=True)  70.9 us
    reduce_scatter x1, waiting for transfers between devices, on_device(): lax.psum_scatter(times_transposed(d_projected, piece).astype(jnp.bfloat16...  64.3 us
    all_gather x1, waiting for transfers between devices, on_device(): cot_all = lax.all_gather(cotangent[0], 'seq', axis=0, tiled=True)  54 us
    all_gather x1, waiting for transfers between devices, on_device(): lax.all_gather(input_weight, 'cand', axis=0, tiled=True)  34.3 us
    all_gather x1, blocking collectives, on_device(): modulation = lax.all_gather(mod_mine, 'seq', axis=1, tiled=True)[0]  31.6 us
    all_gather x1, waiting for transfers between devices, on_device(): w_heads = lax.all_gather(output_weight, 'cand', axis=2, tiled=True)  16.7 us
    all_gather x1, waiting for transfers between devices, on_device(): latent_all = lax.all_gather(latent[0], 'seq', axis=0, tiled=True)  10.1 us
    unnamed x68, local copies, waits for them, and re-layouts  9.94 us
  transfers between devices with their start and end apart: 6, of which 6 were waited for; matrix products, arithmetic and copies ran while one was open for 4% of the time, Pallas kernels for 0%

commit v1 on v0

--- a/solution.py
+++ b/solution.py
@@ -158,7 +158,12 @@
     modulated = (normed_all * (1.0 + scale_vec) + shift_vec).astype(jnp.bfloat16)
     tables = rope_tables(positions, HEAD)
     piece = lax.all_gather(input_weight, "cand", axis=0, tiled=True).reshape(width, group_cols)
-    cot_all = lax.all_gather(cotangent[0], "seq", axis=0, tiled=True)
+    ring = [cotangent[0]]
+    for hop in range(7):
+        ring.append(lax.ppermute(ring[-1], "seq", [(dev, (dev + 1) % 8) for dev in range(8)]))
+    cot_all = jnp.roll(
+        jnp.concatenate(ring[::-1], axis=0), (lax.axis_index("seq") + 1) * ring[0].shape[0], axis=0
+    )
     w_heads = lax.all_gather(output_weight, "cand", axis=2, tiled=True)
     w_heads = w_heads.reshape(w_heads.shape[0] * w_heads.shape[1], width)
     projected = jnp.dot(modulated, piece, preferred_element_type=jnp.float32)

time: 381 us -> 346 us (0.908)
  waiting for transfers between devices: 253 us -> 188 us
  local copies, waits for them, and re-layouts: 33.8 us -> 54.3 us
  other arithmetic: 13.7 us -> 20.8 us
  starting transfers between devices: 0.23 us -> 5.45 us
    all_gather x1 -> x0, waiting for transfers between devices: 54 us -> none  [on_device(): cot_all = lax.all_gather(cotangent[0], 'seq', axis=0, tiled=True)]
    ppermute x0 -> x7, waiting for transfers between devices: none -> 53.7 us  [on_device(): lax.ppermute(ring[-1], 'seq', [(dev, (dev + 1) % 8) for dev in range(8)])]
    all_gather x1, waiting for transfers between devices: 34.3 us -> 0.02 us  [on_device(): lax.all_gather(input_weight, 'cand', axis=0, tiled=True)]
    all_gather x1, waiting for transfers between devices: 16.7 us -> 0.01 us  [on_device(): w_heads = lax.all_gather(output_weight, 'cand', axis=2, tiled=True)]
    unnamed x68 -> x55, local copies, waits for them, and re-layouts: 9.94 us -> 24.5 us
    all_gather x1, waiting for transfers between devices: 10.1 us -> 0.02 us  [on_device(): latent_all = lax.all_gather(latent[0], 'seq', axis=0, tiled=True)]
    ppermute x0 -> x7, starting transfers between devices: none -> 5.26 us  [on_device(): lax.ppermute(ring[-1], 'seq', [(dev, (dev + 1) % 8) for dev in range(8)])]
    concatenate x1, local copies, waits for them, and re-layouts: 0.32 us -> 5.26 us  [rope_tables(): angles = jnp.concatenate(pieces, axis=1)]
  transfers between devices with their start and end apart: 6 -> 12, of which waited for: 6 -> 8; matrix products, arithmetic and copies ran while one was open for 4% -> 13% of each run, Pallas kernels for 0% -> 0%
where the time goes in v1:
time: 346 us; the launch traced here: 345 us
  waiting for transfers between devices  188 us (54%)
  local copies, waits for them, and re-layouts  54.3 us (16%)
  blocking collectives  37 us (11%)
  matrix products  24.4 us (7%)
  other arithmetic  20.8 us (6%)
  between operations  14.1 us (4%)
  starting transfers between devices  5.45 us (2%)
    reduce_scatter x1, waiting for transfers between devices, on_device(): lax.psum_scatter(mixed_part, 'seq', scatter_dimension=0, tiled=True)  70.9 us
    reduce_scatter x1, waiting for transfers between devices, on_device(): lax.psum_scatter(times_transposed(d_projected, piece).astype(jnp.bfloat16...  62.3 us
    ppermute x7, waiting for transfers between devices, on_device(): lax.ppermute(ring[-1], 'seq', [(dev, (dev + 1) % 8) for dev in range(8)])  53.7 us
    all_gather x1, blocking collectives, on_device(): modulation = lax.all_gather(mod_mine, 'seq', axis=1, tiled=True)[0]  31.2 us
    unnamed x55, local copies, waits for them, and re-layouts  24.5 us
  transfers between devices with their start and end apart: 12, of which 8 were waited for; matrix products, arithmetic and copies ran while one was open for 13% of the time, Pallas kernels for 0%

profile of v1, /device:TPU:0, one launch (start us, length us, event | category | flops | bytes accessed | tf_op | source)
XLA Modules:
  0.0 344.5 jit_solution(6128116248542293922)
XLA Ops:
  8.7 3.0 collective-permute-start
  12.5 9.5 %collective-permute-done = bf16[48,3072]{1,0:T(8,128)(2,1)S(1)} collective-permute-done((bf16[48,3072]{1,0:T(8,128)(2,1)}, bf16[48,3072]{1,0:T(8,128)(2,1)S(1)}, u32[]{:S(2)}, u32[]{:S(2)}) %collective-permute-start) | collective-permute-done | bytes 294944 | tf_op jit(solution)/shard_map/ppermute | solution.py:163
  22.3 10.6 %collective-permute-done.1 = bf16[48,3072]{1,0:T(8,128)(2,1)S(1)} collective-permute-done((bf16[48,3072]{1,0:T(8,128)(2,1)S(1)}, bf16[48,3072]{1,0:T(8,128)(2,1)S(1)}, u32[]{:S(2)}, u32[]{:S(2)}) %collective-permute-start.1) | collective-permute-done | bytes 294944 | tf_op jit(solution)/shard_map/ppermute | solution.py:163
  34.5 5.9 %all-reduce = bf16[4,1152]{1,0:T(4,128)(2,1)S(1)} all-reduce(bf16[4,1152]{1,0:T(4,128)(2,1)S(1)} %convolution_convert_fusion.1), channel_id=3, replica_groups=mesh['cand'=4,'seq'=8] {'cand'}, use_global_device_ids=true, to_apply=%region_0.1.clone | all-reduce | flops 4608 | bytes 18432
  41.0 31.2 %all_gather.12 = f32[1,9216]{1,0:T(1,128)S(1)} all-gather(f32[1,1152]{1,0:T(1,128)S(1)} %dynamic-slice_convert_fusion), channel_id=1, replica_groups=mesh['cand'=4,'seq'=8] {'seq'}, dimensions={1}, use_global_device_ids=true | all-gather | bytes 41472 | tf_op jit(solution)/shard_map/all_gather | solution.py:151
  72.2 2.2 collective-permute-start.3
  75.8 10.7 %collective-permute-done.3 = bf16[48,3072]{1,0:T(8,128)(2,1)S(1)} collective-permute-done((bf16[48,3072]{1,0:T(8,128)(2,1)S(1)}, bf16[48,3072]{1,0:T(8,128)(2,1)S(1)}, u32[]{:S(2)}, u32[]{:S(2)}) %collective-permute-start.3) | collective-permute-done | bytes 294944 | tf_op jit(solution)/shard_map/ppermute | solution.py:163
  86.7 11.5 %collective-permute-done.4 = bf16[48,3072]{1,0:T(8,128)(2,1)} collective-permute-done((bf16[48,3072]{1,0:T(8,128)(2,1)S(1)}, bf16[48,3072]{1,0:T(8,128)(2,1)}, u32[]{:S(2)}, u32[]{:S(2)}) %collective-permute-start.4) | collective-permute-done | bytes 294944 | tf_op jit(solution)/shard_map/ppermute | solution.py:163
  98.3 5.3 %concatenate.21 = f32[384,128]{0,1:T(8,128)} concatenate(f32[384,8]{0,1:T(8,128)S(1)} %broadcast_multiply_fusion.6, f32[384,8]{0,1:T(8,128)S(1)} %broadcast_multiply_fusion.6, f32[384,28]{0,1:T(8,128)S(1)} %get-tuple-element.29, f32[384,28]{0,1:T(8,128)S(1)} %get-tuple-element.29, f32[384,28]{0,1:T(8,128)S(1)} %get-tuple-element.28, f32[384,28]{0,1:T(8,128)S(1)} %get-tuple-element.28), dimensions={1} | concatenate | bytes 393216 | tf_op jit(solution)/shard_map/concatenate | solution.py:38
  105.2 3.0 collective-permute-done.5
  109.7 8.3 %collective-permute-done.6 = bf16[48,3072]{1,0:T(8,128)(2,1)} collective-permute-done((bf16[48,3072]{1,0:T(8,128)(2,1)}, bf16[48,3072]{1,0:T(8,128)(2,1)}, u32[]{:S(2)}, u32[]{:S(2)}) %collective-permute-start.6) | collective-permute-done | bytes 294944 | tf_op jit(solution)/shard_map/ppermute | solution.py:163
  136.6 3.1 fusion.22
  139.8 2.1 convert_reduce_fusion
  141.9 2.4 fusion.3
  144.4 5.3 %copy.73 = bf16[384,8,2,384]{3,1,2,0:T(8,128)(2,1)} copy(bf16[384,8,2,384]{3,2,1,0:T(2,128)(2,1)} %bitcast.157) | data formatting | bytes 9437184
  149.7 6.7 %copy.42 = bf16[3072,768]{0,1:T(8,128)(2,1)} copy(bf16[3072,768]{1,0:T(8,128)(2,1)} %bitcast.153) | data formatting | bytes 9437184 | tf_op jit(solution)/shard_map/reshape | solution.py:160
  156.3 5.5 %fusion.17 = f32[3,2,384,128]{2,3,0,1:T(8,128)S(1)} fusion(bf16[2,3,128,3072]{3,2,1,0:T(8,128)(2,1)} %bitcast.158, bf16[1,384,3072]{2,1,0:T(8,128)(2,1)} %all-gather.9.cloned.1.call-done, f32[3072]{0:T(1024)S(1)} %bitcast.169, f32[3072]{0:T(1024)S(1)} %bitcast.164, f32[384]{0:T(512)S(1)} %add_rsqrt_fusion.2, f32[384]{0:T(512)S(1)} %broadcast_multiply_fusion.9), kind=kOutput, calls=%fused_computation.26 | convolution fusion | flops 1819017216 | bytes 8285184 | tf_op jit(solution)/shard_map/dot_general | solution.py:169
  165.6 2.0 gather_fusion.1
  167.6 2.7 gather_fusion
  170.3 1.9 fusion.42
  172.3 2.1 multiply_reduce_fusion
  174.4 2.0 fusion.24
  181.3 2.7 gather_fusion.2
  184.0 2.0 copy.58
  186.1 2.7 gather_fusion.3
  188.8 2.0 multiply_reduce_fusion.2
  190.9 2.0 fusion.51
  193.1 3.5 %convolution_convert_fusion = bf16[384,3072]{1,0:T(8,128)(2,1)} fusion(bf16[384,768]{0,1:T(8,128)(2,1)S(1)} %bitcast.163, bf16[3072,768]{1,0:T(8,128)(2,1)S(1)} %bitcast.156), kind=kOutput, calls=%fused_computation.15 | convolution fusion | flops 1813118976 | bytes 7667712 | tf_op jit(solution)/shard_map/dot_general | solution.py:81
  196.7 4.0 %bitcast_convert_fusion = bf16[384,3072]{1,0:T(8,128)(2,1)} fusion(bf16[2,128,3072]{2,1,0:T(8,128)(2,1)} %all-gather.7.cloned.1.call-done, f32[2,384,384]{1,2,0:T(8,128)S(1)} %get-tuple-element.31, f32[3,2,384,128]{2,3,0,1:T(8,128)} %copy-done.5), kind=kOutput, calls=%fused_computation.13 | convolution fusion | flops 681050112 | bytes 5308416 | tf_op jit(solution)/shard_map/dot_general | solution.py:171
  201.2 62.3 %reduce-scatter.5.cloned.1.call-done = bf16[48,3072]{1,0:T(8,128)(2,1)} async-done(((bf16[384,3072]{1,0:T(8,128)(2,1)}), bf16[48,3072]{1,0:T(8,128)(2,1)}) %reduce-scatter.5.cloned.1.call-update) | async-done | bytes 294928 | tf_op jit(solution)/shard_map/reduce_scatter | solution.py:178
  264.7 70.9 %reduce-scatter.3.cloned.1.call-done = bf16[48,3072]{1,0:T(8,128)(2,1)} async-done(((bf16[384,3072]{1,0:T(8,128)(2,1)}), bf16[48,3072]{1,0:T(8,128)(2,1)}) %reduce-scatter.3.cloned.1.call-update) | async-done | bytes 294928 | tf_op jit(solution)/shard_map/reduce_scatter | solution.py:172
  335.6 2.4 fusion.35
  (112 shorter events, 38.7 us)
Async XLA Ops:
  7.2 25.7 %copy-start = (bf16[768,1152]{1,0:T(8,128)(2,1)S(1)}, bf16[768,1152]{1,0:T(8,128)(2,1)}, u32[]{:S(2)}) copy-start(bf16[768,1152]{1,0:T(8,128)(2,1)} %param.16) | copy-start | bytes 5308420
  7.2 129.4 %all-gather.7.cloned.1.call-start = ((), (), s32[]{:S(2)}) async-start(), calls=%async_computation.3 | async-start | bytes 1966080 | tf_op jit(solution)/shard_map/all_gather | solution.py:167
  7.9 131.9 %all-gather.9.cloned.1.call-start = ((), (), s32[]{:S(2)}) async-start(), calls=%async_computation.6 | async-start | bytes 2654208 | tf_op jit(solution)/shard_map/all_gather | solution.py:155
  8.7 118.4 %copy-start.6 = (bf16[1,48,3072]{2,1,0:T(8,128)(2,1)S(1)}, bf16[1,48,3072]{2,1,0:T(8,128)(2,1)}, u32[]{:S(2)}) copy-start(bf16[1,48,3072]{2,1,0:T(8,128)(2,1)} %param.19) | copy-start | bytes 884740
  8.7 135.7 %all-gather.5.cloned.1.call-start = ((), (), s32[]{:S(2)}) async-start(), calls=%async_computation.2 | async-start | bytes 5898240 | tf_op jit(solution)/shard_map/all_gather | solution.py:160
  8.7 13.3 %collective-permute-start = (bf16[48,3072]{1,0:T(8,128)(2,1)}, bf16[48,3072]{1,0:T(8,128)(2,1)S(1)}, u32[]{:S(2)}, u32[]{:S(2)}) collective-permute-start(bf16[48,3072]{1,0:T(8,128)(2,1)} %bitcast.159), channel_id=1, source_target_pairs={{0,1},{1,2},{2,3},{3,4},{4,5},{5,6},{6,7},{7,0},{8,9},{9,10},{10,1... | collective-permute-start | bytes 884744 | tf_op jit(solution)/shard_map/ppermute | solution.py:163
  11.8 251.7 %reduce-scatter.5.cloned.1.call-start = ((), (), s32[]{:S(2)}) async-start(), calls=%async_computation.5 | async-start | bytes 2654208 | tf_op jit(solution)/shard_map/reduce_scatter | solution.py:178
  22.0 10.9 %collective-permute-start.1 = (bf16[48,3072]{1,0:T(8,128)(2,1)S(1)}, bf16[48,3072]{1,0:T(8,128)(2,1)S(1)}, u32[]{:S(2)}, u32[]{:S(2)}) collective-permute-start(bf16[48,3072]{1,0:T(8,128)(2,1)S(1)} %collective-permute-done), channel_id=1, source_target_pairs={{0,1},{1,2},{2,3},{3,4},{4,5},{5,6},{6,7},{7,0},{8,9},{9,10},{10,1... | collective-permute-start | bytes 884744 | tf_op jit(solution)/shard_map/ppermute | solution.py:163
  32.9 39.3 %collective-permute-start.2 = (bf16[48,3072]{1,0:T(8,128)(2,1)S(1)}, bf16[48,3072]{1,0:T(8,128)(2,1)S(1)}, u32[]{:S(2)}, u32[]{:S(2)}) collective-permute-start(bf16[48,3072]{1,0:T(8,128)(2,1)S(1)} %collective-permute-done.1), channel_id=1, source_target_pairs={{0,1},{1,2},{2,3},{3,4},{4,5},{5,6},{6,7},{7,0},{8,9},{9,10},{10,1... | collective-permute-start | bytes 884744 | tf_op jit(solution)/shard_map/ppermute | solution.py:163
  72.2 14.4 %collective-permute-start.3 = (bf16[48,3072]{1,0:T(8,128)(2,1)S(1)}, bf16[48,3072]{1,0:T(8,128)(2,1)S(1)}, u32[]{:S(2)}, u32[]{:S(2)}) collective-permute-start(bf16[48,3072]{1,0:T(8,128)(2,1)S(1)} %collective-permute-done.2), channel_id=1, source_target_pairs={{0,1},{1,2},{2,3},{3,4},{4,5},{5,6},{6,7},{7,0},{8,9},{9,10},{10,1... | collective-permute-start | bytes 884744 | tf_op jit(solution)/shard_map/ppermute | solution.py:163
  86.6 11.7 %copy-start.7 = (bf16[48,3072]{1,0:T(8,128)(2,1)}, bf16[48,3072]{1,0:T(8,128)(2,1)S(1)}, u32[]{:S(2)}) copy-start(bf16[48,3072]{1,0:T(8,128)(2,1)S(1)} %collective-permute-done.3) | copy-start | bytes 884740
  86.6 11.6 %collective-permute-start.4 = (bf16[48,3072]{1,0:T(8,128)(2,1)S(1)}, bf16[48,3072]{1,0:T(8,128)(2,1)}, u32[]{:S(2)}, u32[]{:S(2)}) collective-permute-start(bf16[48,3072]{1,0:T(8,128)(2,1)S(1)} %collective-permute-done.3), channel_id=1, source_target_pairs={{0,1},{1,2},{2,3},{3,4},{4,5},{5,6},{6,7},{7,0},{8,9},{9,10},{10,1... | collective-permute-start | bytes 884744 | tf_op jit(solution)/shard_map/ppermute | solution.py:163
  98.2 10.1 %collective-permute-start.5 = (bf16[48,3072]{1,0:T(8,128)(2,1)}, bf16[48,3072]{1,0:T(8,128)(2,1)}, u32[]{:S(2)}, u32[]{:S(2)}) collective-permute-start(bf16[48,3072]{1,0:T(8,128)(2,1)} %collective-permute-done.4), channel_id=1, source_target_pairs={{0,1},{1,2},{2,3},{3,4},{4,5},{5,6},{6,7},{7,0},{8,9},{9,10},{10,1... | collective-permute-start | bytes 884744 | tf_op jit(solution)/shard_map/ppermute | solution.py:163
  108.3 9.7 %collective-permute-start.6 = (bf16[48,3072]{1,0:T(8,128)(2,1)}, bf16[48,3072]{1,0:T(8,128)(2,1)}, u32[]{:S(2)}, u32[]{:S(2)}) collective-permute-start(bf16[48,3072]{1,0:T(8,128)(2,1)} %collective-permute-done.5), channel_id=1, source_target_pairs={{0,1},{1,2},{2,3},{3,4},{4,5},{5,6},{6,7},{7,0},{8,9},{9,10},{10,1... | collective-permute-start | bytes 884744 | tf_op jit(solution)/shard_map/ppermute | solution.py:163
  108.9 23.9 %copy-start.8 = (bf16[48,3072]{1,0:T(8,128)(2,1)S(1)}, bf16[48,3072]{1,0:T(8,128)(2,1)}, u32[]{:S(2)}) copy-start(bf16[48,3072]{1,0:T(8,128)(2,1)} %copy-done.7) | copy-start | bytes 884740
  109.7 26.9 %copy-start.13 = (f32[1,3072]{1,0:T(1,128)S(1)}, f32[1,3072]{1,0:T(1,128)}, u32[]{:S(2)}) copy-start(f32[1,3072]{1,0:T(1,128)} %get-tuple-element.23) | copy-start | bytes 36868
  139.8 22.2 %copy-start.9 = (bf16[384,256]{0,1:T(8,128)(2,1)}, bf16[384,256]{0,1:T(8,128)(2,1)S(1)}, u32[]{:S(2)}) copy-start(bf16[384,256]{0,1:T(8,128)(2,1)S(1)} %fusion.22) | copy-start | bytes 589828
  149.7 6.7 %copy-start.15 = (f32[1,3072]{1,0:T(1,128)S(1)}, f32[1,3072]{1,0:T(1,128)}, u32[]{:S(2)}) copy-start(f32[1,3072]{1,0:T(1,128)} %get-tuple-element.24) | copy-start | bytes 36868
  161.8 1.5 copy-start.5
  161.8 8.5 %copy-start.16 = (f32[128]{0:T(128)S(1)}, f32[128]{0:T(128)}, u32[]{:S(2)}) copy-start(f32[128]{0:T(128)} %constant.92.clone) | copy-start | bytes 1540
  163.4 8.8 %copy-start.2 = (f32[2,384,128]{1,2,0:T(8,128)}, f32[2,384,128]{1,2,0:T(8,128)S(1)}, u32[]{:S(2)}) copy-start(f32[2,384,128]{1,2,0:T(8,128)S(1)} %get-tuple-element.12) | copy-start | bytes 1179652
  163.4 16.8 %copy-start.1 = (f32[2,384,128]{1,2,0:T(8,128)}, f32[2,384,128]{1,2,0:T(8,128)S(1)}, u32[]{:S(2)}) copy-start(f32[2,384,128]{1,2,0:T(8,128)S(1)} %get-tuple-element.11) | copy-start | bytes 1179652
  174.3 4.6 %copy-start.11 = (bf16[2,384,128]{1,2,0:T(8,128)(2,1)S(1)}, bf16[2,384,128]{1,2,0:T(8,128)(2,1)}, u32[]{:S(2)}) copy-start(bf16[2,384,128]{1,2,0:T(8,128)(2,1)} %get-tuple-element.14) | copy-start | bytes 589828
  174.3 4.6 %copy-start.12 = (f32[384,128]{0,1:T(8,128)S(1)}, f32[384,128]{0,1:T(8,128)}, u32[]{:S(2)}) copy-start(f32[384,128]{0,1:T(8,128)} %get-tuple-element.35) | copy-start | bytes 589828
  179.0 1.3 copy-start.4
  180.2 12.8 %slice-start = ((s8[4718592]{0:T(1024)(128)(4,1)}), s8[524288]{0:T(1024)(128)(4,1)S(1)}, s32[]{:S(2)}) async-start(s8[4718592]{0:T(1024)(128)(4,1)} %bitcast.154), calls=%async_computation.7 | async-start | bytes 1048576
  188.8 4.1 %copy-start.10 = (bf16[1,2,384,128]{2,3,1,0:T(8,128)(2,1)S(1)}, bf16[1,2,384,128]{2,3,1,0:T(8,128)(2,1)}, u32[]{:S(2)}) copy-start(bf16[1,2,384,128]{2,3,1,0:T(8,128)(2,1)} %fusion.24) | copy-start | bytes 589828
  188.8 4.3 %slice-start.1 = ((s8[4718592]{0:T(1024)(128)(4,1)}), s8[4194304]{0:T(1024)(128)(4,1)S(1)}, s32[]{:S(2)}) async-start(s8[4718592]{0:T(1024)(128)(4,1)} %bitcast.154), calls=%async_computation.8 | async-start | bytes 8388608
  196.6 4.1 %copy-start.3 = (bf16[1,48,3072]{2,1,0:T(8,128)(2,1)S(1)}, bf16[1,48,3072]{2,1,0:T(8,128)(2,1)}, u32[]{:S(2)}) copy-start(bf16[1,48,3072]{2,1,0:T(8,128)(2,1)} %param.13) | copy-start | bytes 884740
  196.6 139.0 %copy-start.14 = (f32[1,3072]{1,0:T(1,128)S(1)}, f32[1,3072]{1,0:T(1,128)}, u32[]{:S(2)}) copy-start(f32[1,3072]{1,0:T(1,128)} %get-tuple-element.23) | copy-start | bytes 36868
  196.6 139.0 %reduce-scatter.3.cloned.1.call-start = ((), (), s32[]{:S(2)}) async-start(), calls=%async_computation.4 | async-start | bytes 2654208 | tf_op jit(solution)/shard_map/reduce_scatter | solution.py:172
Sparse Core Ops, SparseCore 0:
  9.5 22.3 all-gather.6
  34.1 55.9 all-gather.8
  91.7 40.4 all-gather.4
  196.8 66.6 reduce-scatter.4
  266.8 68.7 reduce-scatter.2
